TPU v7x, 256 devices: a whole 4x4x8 slice. The times are simulated.
256 devices in a mesh: row: 16 (over z, core), col: 16 (over y, x).
Axes of the slice: x: 4, y: 4, z: 8, core: 2. Of those that a mesh axis runs over, the one named last changes fastest.
Arguments:
- start_block: float32 [4096, 64, 128], P(('row', 'col')), may hold values from -2700 to 2700
- tile_values: bfloat16 [65536, 128, 128], P(('row', 'col')), may hold values from -3.535534 to 3.535534
- tile_rows: int32 [65536], P(('row', 'col')), may hold values from 0 to 15
- tile_cols: int32 [65536], P(('row', 'col')), may hold values from 0 to 79
- tile_count: int32 [256], P(('row', 'col')), may hold values from 32 to 256, as said below
- send_rows: int32 [256, 256, 32], P(('row', 'col')), may hold values from 0 to 2047
- send_count: int32 [256, 256], P(('row', 'col')), may hold values from 16 to 32, as said below
- rotation: float32 [192, 64], replicated, may hold values from -0.4375 to 0.4375
Outputs:
- embedding: float32 [4096, 64, 128], P(('row', 'col'))
Inputs may be any that keep to these rules, and one draw needn't show every extreme that they name: `tile_cols`: source tiles below 16 are the partition's own row tiles, the others its halo tiles. `tile_count`: slots at or past the count are ignored; some partition fills all 256 slots. `send_count`: slots at or past the count carry zeros; every partition fills all 32 slots for some peer, and some partition receives 32 rows from every partition.
All inputs are finite; a program needn't handle non-finite values.
Results may differ from a plain program's by a relative error of at most 0.0029.
Values may be sent and summed in bfloat16 or wider, within the bound.
A program may use at most 64 MiB of HBM per device.

v0:
```python
import jax
import jax.numpy as jnp
from jax import lax
from jax.sharding import PartitionSpec as P

HIGHEST_PRECISION = lax.Precision.HIGHEST


def local_inner(left_block, right_block):
    return jnp.einsum("tai,tbi->ab", left_block, right_block, precision=HIGHEST_PRECISION)


def unit_columns(product_block, gram_matrix):
    factor = jnp.linalg.cholesky(gram_matrix)
    inverse = lax.linalg.triangular_solve(
        factor, jnp.eye(factor.shape[0], dtype=jnp.float32), left_side=True, lower=True
    )
    return jnp.einsum("ab,tbi->tai", inverse, product_block, precision=HIGHEST_PRECISION)


def apply_graph(current, tile_values, tile_rows, tile_cols, tile_count, send_rows, send_count):
    row_tiles, block_width, tile_size = current.shape
    rounded = current.astype(jnp.bfloat16)
    node_rows = rounded.transpose(0, 2, 1).reshape(row_tiles * tile_size, block_width)
    targets = send_rows[0]
    partitions, capacity = targets.shape
    chosen = node_rows[targets.reshape(-1)].reshape(partitions, capacity, block_width)
    kept_slots = jnp.arange(capacity, dtype=jnp.int32)[None, :] < send_count[0][:, None]
    chosen = jnp.where(kept_slots[:, :, None], chosen, jnp.zeros_like(chosen))
    outgoing = chosen.reshape(lax.axis_size("row"), lax.axis_size("col"), capacity * block_width)
    incoming = lax.all_to_all(
        lax.all_to_all(outgoing, "row", split_axis=0, concat_axis=0, tiled=True),
        "col",
        split_axis=1,
        concat_axis=1,
        tiled=True,
    )
    halo_count = partitions * capacity // tile_size
    halo_block = incoming.reshape(halo_count, tile_size, block_width).transpose(0, 2, 1)
    source = jnp.concatenate([rounded, halo_block], 0)
    picked = source[tile_cols]
    products = jnp.einsum("kbj,kij->kbi", picked, tile_values, preferred_element_type=jnp.float32)
    slot_total = tile_cols.shape[0]
    live_slots = jnp.arange(slot_total, dtype=jnp.int32) < tile_count[0]
    owner_table = (
        tile_rows[None, :] == jnp.arange(row_tiles, dtype=jnp.int32)[:, None]
    ) & live_slots[None, :]
    return jnp.einsum(
        "rk,kbi->rbi", owner_table.astype(jnp.float32), products, precision=HIGHEST_PRECISION
    )


def body(
    start_block, tile_values, tile_rows, tile_cols, tile_count, send_rows, send_count, rotation
):
    node_total = (
        start_block.shape[0] * start_block.shape[2] * lax.axis_size("row") * lax.axis_size("col")
    )
    start_sum = lax.psum(local_inner(start_block, start_block), ("row", "col"))
    vectors = [unit_columns(start_block, start_sum / node_total)]
    for krylov_step in range(2):
        product_block = apply_graph(
            vectors[-1], tile_values, tile_rows, tile_cols, tile_count, send_rows, send_count
        )
        stacked = jnp.concatenate(vectors, 1)
        coefficients = lax.psum(local_inner(stacked, product_block), ("row", "col")) / node_total
        residual_block = product_block - jnp.einsum(
            "ab,tai->tbi", coefficients, stacked, precision=HIGHEST_PRECISION
        )
        gram_matrix = (
            lax.psum(local_inner(residual_block, residual_block), ("row", "col")) / node_total
        )
        vectors.append(unit_columns(residual_block, gram_matrix))
    all_vectors = jnp.concatenate(vectors, 1)
    return jnp.einsum("jb,tji->tbi", rotation, all_vectors, precision=HIGHEST_PRECISION)


def solution(mesh):
    return jax.shard_map(
        body,
        mesh=mesh,
        in_specs=(
            P(("row", "col"), None, None),
            P(("row", "col"), None, None),
            P(("row", "col")),
            P(("row", "col")),
            P(("row", "col")),
            P(("row", "col"), None, None),
            P(("row", "col"), None),
            P(),
        ),
        out_specs=P(("row", "col"), None, None),
        check_vma=False,
    )
```

profile of v0, /device:TPU:1, one launch (start us, length us, event | category | flops | bytes accessed | tf_op | source)
XLA Modules:
  0.0 668.5 jit_solution(7324829424072807957)
XLA Ops:
  0.0 1.0 copy-done
  1.6 81.5 %psum.35 = f32[64,64]{0,1:T(8,128)S(1)} all-reduce(f32[64,64]{0,1:T(8,128)S(1)} %convolution_bitcast_fusion.8), channel_id=1, replica_groups=mesh['row'=16,'col'=16] {'row','col'}, use_global_device_ids=true, to_apply=%region_0.0 | all-reduce | flops 4096 | bytes 32768 | tf_op jit(solution)/shard_map/psum | solution.py:59
  83.2 5.8 cholesky.59
  90.4 4.9 custom-call.7
  96.8 24.0 %gather_fusion = bf16[8192,64]{1,0:T(8,128)(2,1)S(1)} fusion(bf16[2048,64]{1,0:T(8,128)(2,1)S(1)} %bitcast.92, s32[8192]{0:T(1024)S(1)} %broadcast_clamp_fusion), kind=kCustom, calls=%fused_computation | custom fusion | bytes 2129920 | tf_op jit(solution)/shard_map/gather | solution.py:27
  120.9 2.4 reshape.93
  123.4 2.1 broadcast_in_dim.16
  125.5 1.8 broadcast_in_dim.17
  127.3 1.5 broadcast_select_fusion.1
  128.8 33.5 %all_to_all.20 = bf16[16,16,2048]{2,1,0:T(8,128)(2,1)S(1)} all-to-all(bf16[16,16,2048]{2,1,0:T(8,128)(2,1)S(1)} %broadcast_select_fusion.1), channel_id=1, replica_groups=mesh['row'=16,'col'=16] {'row'}, dimensions={0} | all-to-all | bytes 2097152 | tf_op jit(solution)/shard_map/all_to_all | solution.py:32
  162.3 1.6 copy.49
  163.9 3.9 all-to-all-start.1
  168.7 16.5 %all-to-all-done.1 = bf16[16,16,2048]{2,0,1:T(8,128)(2,1)S(1)} async-done(((bf16[16,16,2048]{2,0,1:T(8,128)(2,1)}), bf16[16,16,2048]{2,0,1:T(8,128)(2,1)S(1)}, u32[]{:S(2)}, u32[]{:S(2)}) %all-to-all-start.1) | async-done | bytes 1048608 | tf_op jit(solution)/shard_map/all_to_all | solution.py:31
  185.3 1.6 copy.50
  186.8 3.3 reshape.94
  190.2 2.1 pad_maximum_fusion
  192.2 10.4 %gather_fusion.1 = bf16[256,64,128]{1,2,0:T(8,128)(2,1)} fusion(bf16[80,64,128]{1,2,0:T(8,128)(2,1)} %pad_maximum_fusion, s32[1024]{0:T(1024)S(1)} %pad_clamp_fusion), kind=kCustom, calls=%fused_computation.1 | custom fusion | bytes 8389632 | tf_op jit(solution)/shard_map/gather | solution.py:41
  202.6 9.7 %fusion.57 = f32[256,64,128]{2,1,0:T(8,128)S(1)} fusion(bf16[256,64,128]{1,2,0:T(8,128)(2,1)} %gather_fusion.1, bf16[256,128,128]{2,1,0:T(8,128)(2,1)} %param.12), kind=kOutput, calls=%fused_computation.100 | convolution fusion | flops 536870912 | bytes 20971520 | tf_op jit(solution)/shard_map/kbj,kij->kbi/dot_general | solution.py:42
  212.3 7.5 %fusion.2 = f32[16,64,128]{2,0,1:T(8,128)S(1)} fusion(f32[256,64,128]{2,1,0:T(8,128)S(1)} %fusion.57, s32[256]{0:T(256)S(1)} %copy-done.6, pred[256]{0:T(512)(128)(4,1)S(1)} %iota_compare_fusion.7), kind=kOutput, calls=%fused_computation.6 | convolution fusion | flops 402661376 | bytes 8914176 | tf_op jit(solution)/shard_map/rk,kbi->rbi/dot_general | solution.py:48
  220.5 72.7 %psum.36 = f32[64,64]{0,1:T(8,128)S(1)} all-reduce(f32[64,64]{0,1:T(8,128)S(1)} %convolution_bitcast_fusion.6), channel_id=1, replica_groups=mesh['row'=16,'col'=16] {'row','col'}, use_global_device_ids=true, to_apply=%region_3.0 | all-reduce | flops 4096 | bytes 32768 | tf_op jit(solution)/shard_map/psum | solution.py:66
  294.2 0.7 convolution_bitcast_fusion.5
  295.0 73.9 %psum.37 = f32[64,64]{0,1:T(8,128)S(1)} all-reduce(f32[64,64]{0,1:T(8,128)S(1)} %convolution_bitcast_fusion.5), channel_id=1, replica_groups=mesh['row'=16,'col'=16] {'row','col'}, use_global_device_ids=true, to_apply=%region_4.0 | all-reduce | flops 4096 | bytes 32768 | tf_op jit(solution)/shard_map/psum | solution.py:71
  369.0 5.8 cholesky.70
  374.9 0.7 compare_reduce_fusion.1
  376.3 4.9 custom-call.8
  381.5 1.6 bitcast_convert_fusion
  383.3 24.0 %gather_fusion.2 = bf16[8192,64]{1,0:T(8,128)(2,1)S(1)} fusion(bf16[2048,64]{1,0:T(8,128)(2,1)S(1)} %bitcast.93, s32[8192]{0:T(1024)S(1)} %broadcast_clamp_fusion), kind=kCustom, calls=%fused_computation.2 | custom fusion | bytes 2129920 | tf_op jit(solution)/shard_map/gather | solution.py:27
  407.4 2.4 reshape.96
  409.8 1.5 broadcast_select_fusion
  411.3 32.6 %all_to_all.21 = bf16[16,16,2048]{2,1,0:T(8,128)(2,1)S(1)} all-to-all(bf16[16,16,2048]{2,1,0:T(8,128)(2,1)S(1)} %broadcast_select_fusion), channel_id=1, replica_groups=mesh['row'=16,'col'=16] {'row'}, dimensions={0} | all-to-all | bytes 2097152 | tf_op jit(solution)/shard_map/all_to_all | solution.py:32
  443.9 1.6 copy.64
  445.5 3.9 all-to-all-start.3
  449.7 18.4 %all-to-all-done.3 = bf16[16,16,2048]{2,0,1:T(8,128)(2,1)S(1)} async-done(((bf16[16,16,2048]{2,0,1:T(8,128)(2,1)}), bf16[16,16,2048]{2,0,1:T(8,128)(2,1)S(1)}, u32[]{:S(2)}, u32[]{:S(2)}) %all-to-all-start.3) | async-done | bytes 1048608 | tf_op jit(solution)/shard_map/all_to_all | solution.py:31
  468.1 1.6 copy.65
  469.7 3.3 reshape.97
  473.0 2.1 pad_maximum_fusion.1
  475.1 10.4 %gather_fusion.3 = bf16[256,64,128]{1,2,0:T(8,128)(2,1)} fusion(bf16[80,64,128]{1,2,0:T(8,128)(2,1)} %pad_maximum_fusion.1, s32[1024]{0:T(1024)S(1)} %pad_clamp_fusion), kind=kCustom, calls=%fused_computation.3 | custom fusion | bytes 8389632 | tf_op jit(solution)/shard_map/gather | solution.py:41
  485.5 9.5 %fusion.58 = f32[256,64,128]{2,1,0:T(8,128)S(1)} fusion(bf16[256,64,128]{1,2,0:T(8,128)(2,1)} %gather_fusion.3, bf16[256,128,128]{2,1,0:T(8,128)(2,1)} %param.12), kind=kOutput, calls=%fused_computation.101 | convolution fusion | flops 536870912 | bytes 20971520 | tf_op jit(solution)/shard_map/kbj,kij->kbi/dot_general | solution.py:42
  495.0 7.5 %fusion = f32[16,64,128]{2,0,1:T(8,128)S(1)} fusion(f32[256,64,128]{2,1,0:T(8,128)S(1)} %fusion.58, s32[256]{0:T(256)S(1)} %copy-done.6, pred[256]{0:T(512)(128)(4,1)S(1)} %iota_compare_fusion.7), kind=kOutput, calls=%fused_computation.4 | convolution fusion | flops 402661376 | bytes 8914176 | tf_op jit(solution)/shard_map/rk,kbi->rbi/dot_general | solution.py:48
  502.5 1.2 convolution_bitcast_fusion.1
  503.7 72.8 %psum.38 = f32[128,64]{0,1:T(8,128)S(1)} all-reduce(f32[128,64]{0,1:T(8,128)S(1)} %convolution_bitcast_fusion.1), channel_id=1, replica_groups=mesh['row'=16,'col'=16] {'row','col'}, use_global_device_ids=true, to_apply=%region_5.8 | all-reduce | flops 8192 | bytes 65536 | tf_op jit(solution)/shard_map/psum | solution.py:66
  576.5 0.7 fusion.13
  577.6 0.7 convolution_bitcast_fusion.3
  578.3 74.5 %psum.39 = f32[64,64]{0,1:T(8,128)S(1)} all-reduce(f32[64,64]{0,1:T(8,128)S(1)} %convolution_bitcast_fusion.3), channel_id=1, replica_groups=mesh['row'=16,'col'=16] {'row','col'}, use_global_device_ids=true, to_apply=%region_6.9 | all-reduce | flops 4096 | bytes 32768 | tf_op jit(solution)/shard_map/psum | solution.py:71
  652.9 5.8 cholesky.81
  660.1 4.9 custom-call.9
  665.3 0.8 convolution_bitcast_fusion
  666.1 1.9 fusion.10
  (56 shorter events, 9.1 us)
Async XLA Ops:
  0.0 1.0 copy-start
  0.0 96.5 %copy-start.5 = (s32[1,256,32]{1,2,0:T(8,128)S(1)}, s32[1,256,32]{1,2,0:T(8,128)}, u32[]{:S(2)}) copy-start(s32[1,256,32]{1,2,0:T(8,128)} %param.16) | copy-start | bytes 98308
  96.8 26.5 %copy-start.7 = (s32[1,256]{1,0:T(1,128)S(1)}, s32[1,256]{1,0:T(1,128)}, u32[]{:S(2)}) copy-start(s32[1,256]{1,0:T(1,128)} %param.17) | copy-start | bytes 3076
  127.3 36.6 %copy-start.3 = (pred[16,16,2048]{2,1,0:T(8,128)(4,1)}, pred[16,16,2048]{2,1,0:T(8,128)(4,1)S(1)}, u32[]{:S(2)}) copy-start(pred[16,16,2048]{2,1,0:T(8,128)(4,1)S(1)} %broadcast_in_dim.17) | copy-start | bytes 1572868
  128.8 39.9 %copy-start.8 = (s32[256]{0:T(256)S(1)}, s32[256]{0:T(256)}, u32[]{:S(2)}) copy-start(s32[256]{0:T(256)} %param.14) | copy-start | bytes 3076
  163.9 21.4 %all-to-all-start.1 = ((bf16[16,16,2048]{2,0,1:T(8,128)(2,1)}), bf16[16,16,2048]{2,0,1:T(8,128)(2,1)S(1)}, u32[]{:S(2)}, u32[]{:S(2)}) async-start(bf16[16,16,2048]{2,0,1:T(8,128)(2,1)} %copy.49), calls=%async_computation.1 | async-start | bytes 2097152 | tf_op jit(solution)/shard_map/all_to_all | solution.py:31
  202.6 9.7 %copy-start.6 = (s32[256]{0:T(256)S(1)}, s32[256]{0:T(256)}, u32[]{:S(2)}) copy-start(s32[256]{0:T(256)} %param.13) | copy-start | bytes 3076
  445.5 22.6 %all-to-all-start.3 = ((bf16[16,16,2048]{2,0,1:T(8,128)(2,1)}), bf16[16,16,2048]{2,0,1:T(8,128)(2,1)S(1)}, u32[]{:S(2)}, u32[]{:S(2)}) async-start(bf16[16,16,2048]{2,0,1:T(8,128)(2,1)} %copy.64), calls=%async_computation.3 | async-start | bytes 2097152 | tf_op jit(solution)/shard_map/all_to_all | solution.py:31
  495.0 7.5 %copy-start.2 = (f32[16,128,64]{1,2,0:T(8,128)S(1)}, f32[16,128,64]{1,2,0:T(8,128)}, u32[]{:S(2)}) copy-start(f32[16,128,64]{1,2,0:T(8,128)} %get-tuple-element.11) | copy-start | bytes 1572868
  502.5 163.6 %copy-start.4 = (f32[192,64]{0,1:T(8,128)S(1)}, f32[192,64]{0,1:T(8,128)}, u32[]{:S(2)}) copy-start(f32[192,64]{0,1:T(8,128)} %param.18) | copy-start | bytes 147460
  502.5 165.5 %copy-start.1 = (f32[16,64,128]{2,1,0:T(8,128)S(1)}, f32[16,64,128]{2,1,0:T(8,128)}, u32[]{:S(2)}) copy-start(f32[16,64,128]{2,1,0:T(8,128)} %param.11) | copy-start | bytes 1572868
where the time goes:
time: 675 us; the launch traced here: 668 us
  blocking collectives  442 us (65%)
  local copies, waits for them, and re-layouts  93.1 us (14%)
  matrix products  45.1 us (7%)
  other arithmetic  44.5 us (7%)
  waiting for transfers between devices  35 us (5%)
  starting transfers between devices  7.75 us (1%)
    psum x2, blocking collectives, body(): lax.psum(local_inner(residual_block, residual_block), ('row', 'col'))  148 us
    psum x2, blocking collectives, body(): lax.psum(local_inner(stacked, product_block), ('row', 'col')) / node_total  146 us
    psum x1, blocking collectives, body(): start_sum = lax.psum(local_inner(start_block, start_block), ('row', 'col'))  81.5 us
    all_to_all x2, blocking collectives, apply_graph(): lax.all_to_all(outgoing, 'row', split_axis=0, concat_axis=0, tiled=True)  66.1 us
    gather x2, local copies, waits for them, and re-layouts, apply_graph(): node_rows[targets.reshape(-1)].reshape(partitions, capacity, block_width)  48.1 us
    all_to_all x2, waiting for transfers between devices, apply_graph(): lax.all_to_all(lax.all_to_all(outgoing, 'row', split_axis=0, concat_axis=...  35 us
    gather x2, local copies, waits for them, and re-layouts, apply_graph(): picked = source[tile_cols]  20.7 us
    another operation x9, other arithmetic, unit_columns(): factor = jnp.linalg.cholesky(gram_matrix)  19.6 us
  transfers between devices with their start and end apart: 2, of which 2 were waited for; matrix products, arithmetic and copies ran while one was open for 0% of the time, Pallas kernels for 0%

commit v1 on v0

--- a/solution.py
+++ b/solution.py
@@ -4,6 +4,11 @@
 from jax.sharding import PartitionSpec as P
 
 HIGHEST_PRECISION = lax.Precision.HIGHEST
+
+
+def terms_pair(piece_in, link_axis):
+    ready = jax.lax.all_gather(piece_in, link_axis).sum(axis=0)
+    return ready
 
 
 def local_inner(left_block, right_block):
@@ -68,7 +73,7 @@
             "ab,tai->tbi", coefficients, stacked, precision=HIGHEST_PRECISION
         )
         gram_matrix = (
-            lax.psum(local_inner(residual_block, residual_block), ("row", "col")) / node_total
+            terms_pair(local_inner(residual_block, residual_block), ("row", "col")) / node_total
         )
         vectors.append(unit_columns(residual_block, gram_matrix))
     all_vectors = jnp.concatenate(vectors, 1)

time: 675 us -> 777 us (1.15)
  waiting for transfers between devices: 35 us -> 261 us
  blocking collectives: 442 us -> 294 us
  between operations: 1.53 us -> 14.7 us
  other arithmetic: 44.5 us -> 52.6 us
    all_gather x0 -> x2, waiting for transfers between devices: none -> 227 us  [terms_pair(): ready = jax.lax.all_gather(piece_in, link_axis).sum(axis=0)]
    psum x2 -> x0, blocking collectives: 148 us -> none  [body(): lax.psum(local_inner(residual_block, residual_block), ('row', 'col'))]
    reduce_sum x0 -> x2, other arithmetic: none -> 8.09 us  [terms_pair(): ready = jax.lax.all_gather(piece_in, link_axis).sum(axis=0)]
  transfers between devices with their start and end apart: 2 -> 4, of which waited for: 2 -> 4; matrix products, arithmetic and copies ran while one was open for 0% -> 0% of each run, Pallas kernels for 0% -> 0%
where the time goes in v1:
time: 777 us; the launch traced here: 771 us
  blocking collectives  294 us (38%)
  waiting for transfers between devices  261 us (34%)
  local copies, waits for them, and re-layouts  93.7 us (12%)
  other arithmetic  52.6 us (7%)
  matrix products  46 us (6%)
  between operations  14.7 us (2%)
  starting transfers between devices  8.71 us (1%)
    all_gather x2, waiting for transfers between devices, terms_pair(): ready = jax.lax.all_gather(piece_in, link_axis).sum(axis=0)  227 us
    psum x2, blocking collectives, body(): lax.psum(local_inner(stacked, product_block), ('row', 'col')) / node_total  146 us
    psum x1, blocking collectives, body(): start_sum = lax.psum(local_inner(start_block, start_block), ('row', 'col'))  81.5 us
    all_to_all x2, blocking collectives, apply_graph(): lax.all_to_all(outgoing, 'row', split_axis=0, concat_axis=0, tiled=True)  66.4 us
    gather x2, local copies, waits for them, and re-layouts, apply_graph(): node_rows[targets.reshape(-1)].reshape(partitions, capacity, block_width)  48.1 us
    all_to_all x2, waiting for transfers between devices, apply_graph(): lax.all_to_all(lax.all_to_all(outgoing, 'row', split_axis=0, concat_axis=...  34.7 us
    gather x2, local copies, waits for them, and re-layouts, apply_graph(): picked = source[tile_cols]  20.7 us
    another operation x9, other arithmetic, unit_columns(): factor = jnp.linalg.cholesky(gram_matrix)  19.6 us
  transfers between devices with their start and end apart: 4, of which 4 were waited for; matrix products, arithmetic and copies ran while one was open for 0% of the time, Pallas kernels for 0%

profile of v1, /device:TPU:1, one launch (start us, length us, event | category | flops | bytes accessed | tf_op | source)
XLA Modules:
  0.0 770.9 jit_solution(11039408814972921626)
XLA Ops:
  6.5 1.0 copy-done
  8.1 81.5 %psum.21 = f32[64,64]{0,1:T(8,128)S(1)} all-reduce(f32[64,64]{0,1:T(8,128)S(1)} %convolution_bitcast_fusion.8), channel_id=1, replica_groups=mesh['row'=16,'col'=16] {'row','col'}, use_global_device_ids=true, to_apply=%region_0.0 | all-reduce | flops 4096 | bytes 32768 | tf_op jit(solution)/shard_map/psum | solution.py:64
  89.7 5.8 cholesky.59
  96.9 4.9 custom-call.7
  103.4 24.0 %gather_fusion = bf16[8192,64]{1,0:T(8,128)(2,1)S(1)} fusion(bf16[2048,64]{1,0:T(8,128)(2,1)S(1)} %bitcast.94, s32[8192]{0:T(1024)S(1)} %broadcast_clamp_fusion), kind=kCustom, calls=%fused_computation | custom fusion | bytes 2129920 | tf_op jit(solution)/shard_map/gather | solution.py:32
  127.4 2.4 reshape.93
  130.0 2.1 broadcast_in_dim.16
  132.0 1.8 broadcast_in_dim.17
  133.8 1.5 broadcast_select_fusion.1
  135.4 33.5 %all_to_all.20 = bf16[16,16,2048]{2,1,0:T(8,128)(2,1)S(1)} all-to-all(bf16[16,16,2048]{2,1,0:T(8,128)(2,1)S(1)} %broadcast_select_fusion.1), channel_id=1, replica_groups=mesh['row'=16,'col'=16] {'row'}, dimensions={0} | all-to-all | bytes 2097152 | tf_op jit(solution)/shard_map/all_to_all | solution.py:37
  168.8 1.6 copy.45
  170.4 3.7 all-to-all-start.1
  175.3 16.3 %all-to-all-done.1 = bf16[16,16,2048]{2,0,1:T(8,128)(2,1)S(1)} async-done(((bf16[16,16,2048]{2,0,1:T(8,128)(2,1)}), bf16[16,16,2048]{2,0,1:T(8,128)(2,1)S(1)}, u32[]{:S(2)}, u32[]{:S(2)}) %all-to-all-start.1) | async-done | bytes 1048608 | tf_op jit(solution)/shard_map/all_to_all | solution.py:36
  191.6 1.6 copy.46
  193.2 3.3 reshape.94
  196.5 2.1 pad_maximum_fusion
  198.6 10.4 %gather_fusion.1 = bf16[256,64,128]{1,2,0:T(8,128)(2,1)} fusion(bf16[80,64,128]{1,2,0:T(8,128)(2,1)} %pad_maximum_fusion, s32[1024]{0:T(1024)S(1)} %pad_clamp_fusion), kind=kCustom, calls=%fused_computation.1 | custom fusion | bytes 8389632 | tf_op jit(solution)/shard_map/gather | solution.py:46
  209.0 9.5 %fusion.57 = f32[256,64,128]{2,1,0:T(8,128)S(1)} fusion(bf16[256,64,128]{1,2,0:T(8,128)(2,1)} %gather_fusion.1, bf16[256,128,128]{2,1,0:T(8,128)(2,1)} %param.12), kind=kOutput, calls=%fused_computation.100 | convolution fusion | flops 536870912 | bytes 20971520 | tf_op jit(solution)/shard_map/kbj,kij->kbi/dot_general | solution.py:47
  218.5 7.5 fusion.2
  226.7 73.0 %psum.22 = f32[64,64]{0,1:T(8,128)S(1)} all-reduce(f32[64,64]{0,1:T(8,128)S(1)} %convolution_bitcast_fusion.6), channel_id=1, replica_groups=mesh['row'=16,'col'=16] {'row','col'}, use_global_device_ids=true, to_apply=%region_3.0 | all-reduce | flops 4096 | bytes 32768 | tf_op jit(solution)/shard_map/psum | solution.py:71
  300.6 1.3 convolution_bitcast_fusion.5
  301.9 113.4 %all-gather.5.cloned.1.call-done = f32[16384,64]{1,0:T(8,128)} async-done(((f32[64,64]{1,0:T(8,128)}), f32[16384,64]{1,0:T(8,128)}) %all-gather.5.cloned.1.call-update) | async-done | bytes 4194320 | tf_op jit(solution)/shard_map/all_gather | solution.py:10
  415.4 4.0 reduce_sum.18
  419.6 5.8 cholesky.70
  426.9 4.9 custom-call.8
  432.0 1.6 bitcast_convert_fusion
  433.9 24.0 %gather_fusion.2 = bf16[8192,64]{1,0:T(8,128)(2,1)S(1)} fusion(bf16[2048,64]{1,0:T(8,128)(2,1)S(1)} %bitcast.95, s32[8192]{0:T(1024)S(1)} %broadcast_clamp_fusion), kind=kCustom, calls=%fused_computation.2 | custom fusion | bytes 2129920 | tf_op jit(solution)/shard_map/gather | solution.py:32
  458.0 2.4 reshape.96
  460.4 1.5 broadcast_select_fusion
  461.9 32.9 %all_to_all.21 = bf16[16,16,2048]{2,1,0:T(8,128)(2,1)S(1)} all-to-all(bf16[16,16,2048]{2,1,0:T(8,128)(2,1)S(1)} %broadcast_select_fusion), channel_id=1, replica_groups=mesh['row'=16,'col'=16] {'row'}, dimensions={0} | all-to-all | bytes 2097152 | tf_op jit(solution)/shard_map/all_to_all | solution.py:37
  494.8 1.6 copy.60
  496.4 4.8 all-to-all-start.3
  501.6 18.4 %all-to-all-done.3 = bf16[16,16,2048]{2,0,1:T(8,128)(2,1)S(1)} async-done(((bf16[16,16,2048]{2,0,1:T(8,128)(2,1)}), bf16[16,16,2048]{2,0,1:T(8,128)(2,1)S(1)}, u32[]{:S(2)}, u32[]{:S(2)}) %all-to-all-start.3) | async-done | bytes 1048608 | tf_op jit(solution)/shard_map/all_to_all | solution.py:36
  520.0 1.6 copy.61
  521.5 3.8 reshape.97
  525.3 2.1 pad_maximum_fusion.1
  527.4 10.4 %gather_fusion.3 = bf16[256,64,128]{1,2,0:T(8,128)(2,1)} fusion(bf16[80,64,128]{1,2,0:T(8,128)(2,1)} %pad_maximum_fusion.1, s32[1024]{0:T(1024)S(1)} %pad_clamp_fusion), kind=kCustom, calls=%fused_computation.3 | custom fusion | bytes 8389632 | tf_op jit(solution)/shard_map/gather | solution.py:46
  537.7 9.5 %fusion.58 = f32[256,64,128]{2,1,0:T(8,128)S(1)} fusion(bf16[256,64,128]{1,2,0:T(8,128)(2,1)} %gather_fusion.3, bf16[256,128,128]{2,1,0:T(8,128)(2,1)} %param.12), kind=kOutput, calls=%fused_computation.101 | convolution fusion | flops 536870912 | bytes 20971520 | tf_op jit(solution)/shard_map/kbj,kij->kbi/dot_general | solution.py:47
  547.2 7.5 fusion
  554.7 1.2 convolution_bitcast_fusion.1
  555.9 73.0 %psum.23 = f32[128,64]{0,1:T(8,128)S(1)} all-reduce(f32[128,64]{0,1:T(8,128)S(1)} %convolution_bitcast_fusion.1), channel_id=1, replica_groups=mesh['row'=16,'col'=16] {'row','col'}, use_global_device_ids=true, to_apply=%region_5.8 | all-reduce | flops 8192 | bytes 65536 | tf_op jit(solution)/shard_map/psum | solution.py:71
  630.0 1.3 convolution_bitcast_fusion.3
  631.3 113.2 %all-gather.7.cloned.1.call-done = f32[16384,64]{1,0:T(8,128)} async-done(((f32[64,64]{1,0:T(8,128)}), f32[16384,64]{1,0:T(8,128)}) %all-gather.7.cloned.1.call-update) | async-done | bytes 4194320 | tf_op jit(solution)/shard_map/all_gather | solution.py:10
  744.5 4.1 reduce_sum.19
  748.8 5.8 cholesky.81
  755.9 4.9 custom-call.9
  761.1 0.8 convolution_bitcast_fusion
  761.9 1.9 fusion.10
  (64 shorter events, 11.0 us)
Async XLA Ops:
  6.5 1.0 copy-start
  6.5 96.5 %copy-start.5 = (s32[1,256,32]{1,2,0:T(8,128)S(1)}, s32[1,256,32]{1,2,0:T(8,128)}, u32[]{:S(2)}) copy-start(s32[1,256,32]{1,2,0:T(8,128)} %param.16) | copy-start | bytes 98308
  103.3 26.5 %copy-start.7 = (s32[1,256]{1,0:T(1,128)S(1)}, s32[1,256]{1,0:T(1,128)}, u32[]{:S(2)}) copy-start(s32[1,256]{1,0:T(1,128)} %param.17) | copy-start | bytes 3076
  133.8 36.6 %copy-start.3 = (pred[16,16,2048]{2,1,0:T(8,128)(4,1)}, pred[16,16,2048]{2,1,0:T(8,128)(4,1)S(1)}, u32[]{:S(2)}) copy-start(pred[16,16,2048]{2,1,0:T(8,128)(4,1)S(1)} %broadcast_in_dim.17) | copy-start | bytes 1572868
  135.4 39.9 %copy-start.8 = (s32[256]{0:T(256)S(1)}, s32[256]{0:T(256)}, u32[]{:S(2)}) copy-start(s32[256]{0:T(256)} %param.14) | copy-start | bytes 3076
  170.4 21.2 %all-to-all-start.1 = ((bf16[16,16,2048]{2,0,1:T(8,128)(2,1)}), bf16[16,16,2048]{2,0,1:T(8,128)(2,1)S(1)}, u32[]{:S(2)}, u32[]{:S(2)}) async-start(bf16[16,16,2048]{2,0,1:T(8,128)(2,1)} %copy.45), calls=%async_computation.1 | async-start | bytes 2097152 | tf_op jit(solution)/shard_map/all_to_all | solution.py:36
  174.1 241.3 %all-gather.5.cloned.1.call-start = ((), (), s32[]{:S(2)}) async-start(), calls=%async_computation.4 | async-start | bytes 8421376 | tf_op jit(solution)/shard_map/all_gather | solution.py:10
  209.0 9.5 %copy-start.6 = (s32[256]{0:T(256)S(1)}, s32[256]{0:T(256)}, u32[]{:S(2)}) copy-start(s32[256]{0:T(256)} %param.13) | copy-start | bytes 3076
  496.4 23.5 %all-to-all-start.3 = ((bf16[16,16,2048]{2,0,1:T(8,128)(2,1)}), bf16[16,16,2048]{2,0,1:T(8,128)(2,1)S(1)}, u32[]{:S(2)}, u32[]{:S(2)}) async-start(bf16[16,16,2048]{2,0,1:T(8,128)(2,1)} %copy.60), calls=%async_computation.3 | async-start | bytes 2097152 | tf_op jit(solution)/shard_map/all_to_all | solution.py:36
  501.2 243.3 %all-gather.7.cloned.1.call-start = ((), (), s32[]{:S(2)}) async-start(), calls=%async_computation.5 | async-start | bytes 8421376 | tf_op jit(solution)/shard_map/all_gather | solution.py:10
  547.2 7.5 copy-start.2
  744.5 19.3 %copy-start.1 = (f32[16,64,128]{2,1,0:T(8,128)S(1)}, f32[16,64,128]{2,1,0:T(8,128)}, u32[]{:S(2)}) copy-start(f32[16,64,128]{2,1,0:T(8,128)} %param.11) | copy-start | bytes 1572868
  744.5 17.4 %copy-start.4 = (f32[192,64]{0,1:T(8,128)S(1)}, f32[192,64]{0,1:T(8,128)}, u32[]{:S(2)}) copy-start(f32[192,64]{0,1:T(8,128)} %param.18) | copy-start | bytes 147460
Sparse Core Ops, SparseCore 0:
  302.0 113.2 all-gather.4
  631.5 112.9 all-gather.6
